TPU v7x, 128 devices: a whole 4x4x4 slice. The times are simulated.
128 devices in a mesh: row: 8 (over x_hi, y), col: 16 (over x_lo, z, core).
Axes of the slice: x: 4 (x_hi: 2, x_lo: 2; x = x_hi * 2 + x_lo), y: 4, z: 4, core: 2. Of those that a mesh axis runs over, the one named last changes fastest.
Arguments:
- flexibility: bfloat16 [2048, 384, 384], P(('row', 'col'))
- coupling: bfloat16 [2048, 384, 512], P(('row', 'col')), may hold values from -0.3125 to 0.3125
- boundary: bfloat16 [2048, 512, 512], P(('row', 'col'))
- masses: float32 [2048, 384], P(('row', 'col')), may hold values from 0.5 to 2
- start_modes: bfloat16 [2048, 64, 384], P(('row', 'col')), may hold values from -6 to 6
- interior_sizes: int32 [2048], P(('row', 'col')), may hold values from 128 to 384, as said below
- interface: int32 [2048, 4], P(('row', 'col')), may hold values from 0 to 255, as said below
- start_block: float32 [32, 32768], P(None, ('row', 'col')), may hold values from -6 to 6
Outputs:
- alpha_first: float32 [32, 32], replicated
- alpha_second: float32 [32, 32], replicated
- next_block: float32 [32, 32768], P(None, ('row', 'col'))
- residual_block: float32 [32, 32768], P(None, ('row', 'col'))
- mass_coupling: float32 [2048, 64, 512], P(('row', 'col'))
Inputs may be any that keep to these rules, and one draw needn't show every extreme that they name: `interior_sizes`: every device's shard holds a substructure with exactly 384 interior DOFs. `interface`: block id I stands for assembled DOFs 128 I to 128 I + 127; it lies in piece I // 2 of the assembled order, which belongs to row index (I // 2) // (number of col indices) and col index (I // 2) % (number of col indices) of the mesh. The four blocks of one substructure have four different row indices and four different col indices. For every device and every pair of a row index r and a col index c, exactly 2 of the device's 16 substructures have one block at row index r and one block at col index c. Every piece in which some block of a device's substructures lies holds exactly 2 of that device's blocks, counted over its substructures and their four blocks.
All inputs are finite; a program needn't handle non-finite values.
Results may differ from a plain program's by a relative error of at most 0.0083.
Values may be sent and summed in bfloat16 or wider, within the bound.
A program may use at most 192 MiB of HBM per device.

v0:
```python
import math

import jax
import jax.numpy as jnp
from jax import lax
from jax.sharding import PartitionSpec as P

ITERS = 4


HIGHEST = lax.Precision.HIGHEST


def condense(flexibility, coupling, boundary, masses, start_modes, interior_count):
    interior = flexibility.shape[0]
    active = (jnp.arange(interior) < interior_count).astype(jnp.float32)
    weight = masses * active
    modes_now = start_modes.astype(jnp.float32) * active
    for sweep in range(ITERS):
        scaled = (modes_now * weight).astype(jnp.bfloat16)
        applied = jnp.dot(scaled, flexibility, preferred_element_type=jnp.float32) * active
        gram_matrix = jnp.dot(applied * weight, applied.T, precision=HIGHEST)
        factor = jnp.linalg.cholesky(gram_matrix)
        modes_now = jax.scipy.linalg.solve_triangular(factor, applied, lower=True)
    masked = coupling * active.astype(jnp.bfloat16)[:, None]
    flexed = (jnp.dot(masked.T, flexibility, preferred_element_type=jnp.float32) * active).astype(
        jnp.bfloat16
    )
    projected = (modes_now * weight).astype(jnp.bfloat16)
    coupling_modal = jnp.dot(projected, flexed.T, preferred_element_type=jnp.float32)
    condensed = boundary.astype(jnp.float32) - jnp.dot(
        flexed, masked, preferred_element_type=jnp.float32
    )
    return (((condensed + condensed.T) * 0.5).astype(jnp.bfloat16), -coupling_modal)


def on_device(
    flexibility, coupling, boundary, masses, start_modes, interior_sizes, interface, start_block
):
    row_count = lax.axis_size("row")
    col_count = lax.axis_size("col")
    devices = row_count * col_count
    local_subs = flexibility.shape[0]
    tile_edge = boundary.shape[1] // 4
    tile_total = local_subs * 16
    capacity = tile_total // devices
    width = start_block.shape[0]
    tiles, mass_coupling = jax.vmap(condense)(
        flexibility, coupling, boundary, masses, start_modes, interior_sizes
    )
    tile_grid = tiles.reshape(local_subs, 4, tile_edge, 4, tile_edge).transpose(0, 1, 3, 2, 4)
    ref_count = local_subs * 4
    ref_ids = interface.reshape(ref_count)
    ref_owner = ref_ids // 2
    ref_order = jnp.arange(ref_count)
    ahead = (ref_owner[None, :] == ref_owner[:, None]) & (ref_order[None, :] < ref_order[:, None])
    ref_slot = ref_owner * capacity + jnp.sum(ahead.astype(jnp.int32), axis=1)
    slot_total = devices * capacity
    request = jnp.zeros((slot_total,), jnp.int32).at[ref_slot].set(ref_ids)
    asked_ids = lax.all_to_all(request, ("row", "col"), split_axis=0, concat_axis=0, tiled=True)
    parity_pick = ((asked_ids % 2)[:, None] == jnp.arange(2)[None, :]).astype(jnp.float32)
    wide_tiles = tile_grid.astype(jnp.float32)

    def apply_matrix(vectors):
        local_pair = vectors.reshape(width, 2, tile_edge)
        reply = jnp.einsum("kp,xpt->kxt", parity_pick, local_pair, precision=HIGHEST)
        returned = lax.all_to_all(reply, ("row", "col"), split_axis=0, concat_axis=0, tiled=True)
        gathered = returned[ref_slot].reshape(local_subs, 4, width, tile_edge)
        product_terms = jnp.einsum("saxt,sabtu->sbxu", gathered, wide_tiles, precision=HIGHEST)
        outgoing = (
            jnp.zeros((slot_total, width, tile_edge), jnp.float32)
            .at[ref_slot]
            .set(product_terms.reshape(ref_count, width, tile_edge))
        )
        incoming = lax.all_to_all(
            outgoing.astype(jnp.bfloat16), ("row", "col"), split_axis=0, concat_axis=0, tiled=True
        ).astype(outgoing.dtype)
        result = jnp.einsum("kp,kxt->xpt", parity_pick, incoming, precision=HIGHEST)
        return result.reshape(width, 2 * tile_edge)

    gram_start = lax.psum(jnp.dot(start_block, start_block.T, precision=HIGHEST), ("row", "col"))
    first_block = jax.scipy.linalg.solve_triangular(
        jnp.linalg.cholesky(gram_start), start_block, lower=True
    )
    applied_first = apply_matrix(first_block)
    alpha_first = lax.psum(jnp.dot(applied_first, first_block.T, precision=HIGHEST), ("row", "col"))
    remainder = applied_first - jnp.dot(alpha_first, first_block, precision=HIGHEST)
    gram_rest = lax.psum(jnp.dot(remainder, remainder.T, precision=HIGHEST), ("row", "col"))
    beta_factor = jnp.linalg.cholesky(gram_rest)
    second_block = jax.scipy.linalg.solve_triangular(beta_factor, remainder, lower=True)
    applied_second = apply_matrix(second_block) - jnp.dot(
        beta_factor.T, first_block, precision=HIGHEST
    )
    alpha_second = lax.psum(
        jnp.dot(applied_second, second_block.T, precision=HIGHEST), ("row", "col")
    )
    leftover = applied_second - jnp.dot(alpha_second, second_block, precision=HIGHEST)
    rescale = math.sqrt(devices * start_block.shape[1])
    return (alpha_first, alpha_second, rescale * second_block, rescale * leftover, mass_coupling)


def solution(mesh):
    return jax.shard_map(
        on_device,
        mesh=mesh,
        in_specs=(
            P(("row", "col"), None, None),
            P(("row", "col"), None, None),
            P(("row", "col"), None, None),
            P(("row", "col"), None),
            P(("row", "col"), None, None),
            P(("row", "col")),
            P(("row", "col"), None),
            P(None, ("row", "col")),
        ),
        out_specs=(
            P(),
            P(),
            P(None, ("row", "col")),
            P(None, ("row", "col")),
            P(("row", "col"), None, None),
        ),
        check_vma=False,
    )
```

profile of v0, /device:TPU:1, one launch (start us, length us, event | category | flops | bytes accessed | tf_op | source)
XLA Modules:
  0.0 1199.0 jit_solution(16197807236306925908)
XLA Ops:
  3.4 11.5 all-to-all-start
  15.0 67.3 %psum.28 = f32[32,32]{0,1:T(8,128)S(1)} all-reduce(f32[32,32]{0,1:T(8,128)S(1)} %fusion.75), channel_id=1, replica_groups=mesh['row'=8,'col'=16] {'row','col'}, use_global_device_ids=true, to_apply=%region_2.3 | all-reduce | flops 1024 | bytes 8192 | tf_op jit(solution)/shard_map/psum | solution.py:81
  93.4 4.4 copy.77
  97.8 6.0 all-to-all-start.1
  103.9 11.9 multiply_convert_fusion
  115.8 17.3 %convert_subtract_fusion = f32[16,512,512]{2,1,0:T(8,128)} fusion(bf16[16,512,512]{2,1,0:T(8,128)(2,1)} %param.16, bf16[16,512,384]{2,1,0:T(8,128)(2,1)} %multiply_convert_fusion, bf16[16,384,512]{2,1,0:T(8,128)(2,1)} %param.15, bf16[16,384]{1,0:T(8,128)(2,1)S(1)} %get-tuple-element.9), kind=kOutput, calls=%fused_computation.8 | convolution fusion | flops 3232759808 | bytes 37761024 | tf_op jit(solution)/shard_map/vmap()/dot_general | solution.py:31
  133.1 17.6 %copy.72 = f32[16,512,512]{1,2,0:T(8,128)} copy(f32[16,512,512]{2,1,0:T(8,128)} %convert_subtract_fusion) | data formatting | bytes 33554432 | tf_op jit(solution)/shard_map/vmap()/sub | solution.py:31
  150.7 14.9 %fusion.1 = bf16[16,512,512]{2,1,0:T(8,128)(2,1)} fusion(f32[16,512,512]{2,1,0:T(8,128)} %convert_subtract_fusion, f32[16,512,512]{1,2,0:T(8,128)} %copy.72), kind=kLoop, calls=%fused_computation.7 | loop fusion | flops 12582912 | bytes 41943040 | tf_op jit(solution)/shard_map/vmap()/convert_element_type | solution.py:34
  165.6 12.5 %reshape.250 = bf16[16,4,128,4,128]{4,3,2,1,0:T(4,128)(2,1)} reshape(bf16[16,512,512]{2,1,0:T(8,128)(2,1)} %fusion.1) | data formatting | bytes 16777216 | tf_op jit(solution)/shard_map/reshape | solution.py:51
  181.0 7.7 fusion.4
  191.2 8.1 scatter_fusion
  199.4 4.0 convert_element_type.64
  203.4 10.4 all-to-all-start.2
  219.3 93.8 %custom-call.20 = f32[16,64,64]{2,1,0:T(8,128)S(1)} custom-call(f32[16,64,64]{2,1,0:T(8,128)S(1)} %fusion.41), custom_call_target="Cholesky" | custom-call | tf_op jit(solution)/shard_map/vmap(jit(cholesky))/cholesky | solution.py:23
  315.7 67.3 %psum.29 = f32[32,32]{1,0:T(8,128)S(1)} all-reduce(f32[32,32]{1,0:T(8,128)S(1)} %fusion.42), channel_id=1, replica_groups=mesh['row'=8,'col'=16] {'row','col'}, use_global_device_ids=true, to_apply=%region_6.9 | all-reduce | flops 1024 | bytes 8192 | tf_op jit(solution)/shard_map/psum | solution.py:86
  383.3 63.0 %psum.30 = f32[32,32]{0,1:T(8,128)S(1)} all-reduce(f32[32,32]{0,1:T(8,128)S(1)} %fusion.76), channel_id=1, replica_groups=mesh['row'=8,'col'=16] {'row','col'}, use_global_device_ids=true, to_apply=%region_7.10 | all-reduce | flops 1024 | bytes 8192 | tf_op jit(solution)/shard_map/psum | solution.py:88
  455.8 4.4 copy.81
  460.2 5.8 all-to-all-start.3
  466.1 78.6 %custom-call.21 = f32[16,1,64,64]{2,3,1,0:T(8,128)S(1)} custom-call(f32[16,1,64,64]{3,2,1,0:T(8,128)S(1)} %select_bitcast_fusion.3), custom_call_target="InvertDiagBlocksLowerTriangular" | custom-call | tf_op jit(solution)/shard_map/vmap(jit(_solve_triangular))/triangular_solve | solution.py:24
  546.4 3.3 convolution_multiply_fusion.2
  551.9 93.8 %custom-call.22 = f32[16,64,64]{2,1,0:T(8,128)S(1)} custom-call(f32[16,64,64]{2,1,0:T(8,128)S(1)} %fusion.39), custom_call_target="Cholesky" | custom-call | tf_op jit(solution)/shard_map/vmap(jit(cholesky))/cholesky | solution.py:23
  646.0 78.8 %custom-call.23 = f32[16,1,64,64]{2,3,1,0:T(8,128)S(1)} custom-call(f32[16,1,64,64]{3,2,1,0:T(8,128)S(1)} %select_bitcast_fusion.2), custom_call_target="InvertDiagBlocksLowerTriangular" | custom-call | tf_op jit(solution)/shard_map/vmap(jit(_solve_triangular))/triangular_solve | solution.py:24
  731.9 93.8 %custom-call.24 = f32[16,64,64]{2,1,0:T(8,128)S(1)} custom-call(f32[16,64,64]{2,1,0:T(8,128)S(1)} %fusion.37), custom_call_target="Cholesky" | custom-call | tf_op jit(solution)/shard_map/vmap(jit(cholesky))/cholesky | solution.py:23
  826.0 78.6 %custom-call.25 = f32[16,1,64,64]{2,3,1,0:T(8,128)S(1)} custom-call(f32[16,1,64,64]{3,2,1,0:T(8,128)S(1)} %select_bitcast_fusion.1), custom_call_target="InvertDiagBlocksLowerTriangular" | custom-call | tf_op jit(solution)/shard_map/vmap(jit(_solve_triangular))/triangular_solve | solution.py:24
  909.0 7.5 fusion.2
  919.1 8.1 scatter_fusion.1
  927.2 4.0 convert_element_type.65
  931.2 10.2 all-to-all-start.4
  946.9 93.8 %custom-call.26 = f32[16,64,64]{2,1,0:T(8,128)S(1)} custom-call(f32[16,64,64]{2,1,0:T(8,128)S(1)} %fusion.35), custom_call_target="Cholesky" | custom-call | tf_op jit(solution)/shard_map/vmap(jit(cholesky))/cholesky | solution.py:23
  1041.1 78.6 %custom-call.27 = f32[16,1,64,64]{2,3,1,0:T(8,128)S(1)} custom-call(f32[16,1,64,64]{3,2,1,0:T(8,128)S(1)} %select_bitcast_fusion), custom_call_target="InvertDiagBlocksLowerTriangular" | custom-call | tf_op jit(solution)/shard_map/vmap(jit(_solve_triangular))/triangular_solve | solution.py:24
  1121.3 6.2 convolution_negate_fusion
  1130.8 67.3 %psum.31 = f32[32,32]{1,0:T(8,128)S(1)} all-reduce(f32[32,32]{1,0:T(8,128)S(1)} %fusion.77), channel_id=1, replica_groups=mesh['row'=8,'col'=16] {'row','col'}, use_global_device_ids=true, to_apply=%region_9.12 | all-reduce | flops 1024 | bytes 8192 | tf_op jit(solution)/shard_map/psum | solution.py:94
  (108 shorter events, 66.9 us)
Async XLA Ops:
  0.6 14.2 %copy-start = (f32[32,256]{1,0:T(8,128)S(1)}, f32[32,256]{1,0:T(8,128)}, u32[]{:S(2)}) copy-start(f32[32,256]{1,0:T(8,128)} %param.21) | copy-start | bytes 98308
  1.8 189.4 %copy-start.8 = (s32[64]{0:T(128)}, s32[64]{0:T(128)S(1)}, u32[]{:S(2)}) copy-start(s32[64]{0:T(128)S(1)} %fusion.70) | copy-start | bytes 772
  3.4 86.7 %all-to-all-start = ((s32[128,2,1]{1,2,0:T(1,128)}), s32[128,2,1]{1,2,0:T(1,128)S(1)}, u32[]{:S(2)}, u32[]{:S(2)}) async-start(s32[128,2,1]{1,2,0:T(1,128)} %bitcast.4), calls=%async_computation | async-start | bytes 131072 | tf_op jit(solution)/shard_map/all_to_all | solution.py:60
  91.6 362.4 %copy-start.6 = (s32[256]{0:T(256)}, s32[256]{0:T(256)S(1)}, u32[]{:S(2)}) copy-start(s32[256]{0:T(256)S(1)} %and_select_fusion) | copy-start | bytes 3076
  97.8 80.4 %all-to-all-start.1 = ((f32[256,32,128]{2,1,0:T(8,128)}), f32[256,32,128]{2,1,0:T(8,128)}, u32[]{:S(2)}, u32[]{:S(2)}) async-start(f32[256,32,128]{2,1,0:T(8,128)} %copy.77), calls=%async_computation.1 | async-start | bytes 8388608 | tf_op jit(solution)/shard_map/all_to_all | solution.py:67
  203.4 10.4 copy-start.5
  203.4 10.4 copy-start.10
  203.4 10.5 copy-start.2
  203.4 109.9 %all-to-all-start.2 = ((bf16[256,32,128]{2,1,0:T(8,128)(2,1)}), bf16[256,32,128]{2,1,0:T(8,128)(2,1)}, u32[]{:S(2)}, u32[]{:S(2)}) async-start(bf16[256,32,128]{2,1,0:T(8,128)(2,1)} %convert_element_type.64), calls=%async_computation.2 | async-start | bytes 4194304 | tf_op jit(solution)/shard_map/all_to_all | solution.py:75
  383.0 72.8 %copy-start.3 = (f32[32,32]{1,0:T(8,128)}, f32[32,32]{1,0:T(8,128)S(1)}, u32[]{:S(2)}) copy-start(f32[32,32]{1,0:T(8,128)S(1)} %psum.29) | copy-start | bytes 12292
  460.2 446.0 %all-to-all-start.3 = ((f32[256,32,128]{2,1,0:T(8,128)}), f32[256,32,128]{2,1,0:T(8,128)}, u32[]{:S(2)}, u32[]{:S(2)}) async-start(f32[256,32,128]{2,1,0:T(8,128)} %copy.81), calls=%async_computation.3 | async-start | bytes 8388608 | tf_op jit(solution)/shard_map/all_to_all | solution.py:67
  916.6 2.5 copy-start.9
  931.2 196.3 %all-to-all-start.4 = ((bf16[256,32,128]{2,1,0:T(8,128)(2,1)}), bf16[256,32,128]{2,1,0:T(8,128)(2,1)}, u32[]{:S(2)}, u32[]{:S(2)}) async-start(bf16[256,32,128]{2,1,0:T(8,128)(2,1)} %convert_element_type.65), calls=%async_computation.4 | async-start | bytes 4194304 | tf_op jit(solution)/shard_map/all_to_all | solution.py:75
  1121.3 6.3 copy-start.7
  1121.3 77.5 %copy-start.1 = (f32[32,256]{1,0:T(8,128)S(1)}, f32[32,256]{1,0:T(8,128)}, u32[]{:S(2)}) copy-start(f32[32,256]{1,0:T(8,128)} %param.21) | copy-start | bytes 98308
  1198.0 0.8 copy-start.4
where the time goes:
time: 1210 us; the launch traced here: 1200 us
  other arithmetic  729 us (60%)
  blocking collectives  265 us (22%)
  matrix products  89.5 us (7%)
  local copies, waits for them, and re-layouts  69.9 us (6%)
  starting transfers between devices  43.9 us (4%)
    another operation x13, other arithmetic, condense(): factor = jnp.linalg.cholesky(gram_matrix)  376 us
    another operation x9, other arithmetic, condense(): modes_now = jax.scipy.linalg.solve_triangular(factor, applied, lower=True)  315 us
    psum x1, blocking collectives, on_device(): lax.psum(jnp.dot(start_block, start_block.T, precision=HIGHEST), ('row',...  67.3 us
    psum x1, blocking collectives, on_device(): lax.psum(jnp.dot(applied_first, first_block.T, precision=HIGHEST), ('row'...  67.3 us
    psum x1, blocking collectives, on_device(): lax.psum(jnp.dot(applied_second, second_block.T, precision=HIGHEST), ('ro...  67.3 us
    psum x1, blocking collectives, on_device(): lax.psum(jnp.dot(remainder, remainder.T, precision=HIGHEST), ('row', 'col'))  63 us
  transfers between devices with their start and end apart: 5, of which 0 were waited for; matrix products, arithmetic and copies ran while one was open for 67% of the time, Pallas kernels for 0%

commit v1 on v0

v1 whole, which is shorter than its diff:
```python
import functools
import math

import jax
import jax.numpy as jnp
from jax import lax
from jax.experimental import pallas as pl
from jax.experimental.pallas import tpu as pltpu
from jax.sharding import PartitionSpec as P

ITERS = 4
HIGHEST = lax.Precision.HIGHEST
F32 = jnp.float32
BF16 = jnp.bfloat16


def dot(a, b, ca=1, cb=0, precision=None):
    return lax.dot_general(
        a, b, (((ca,), (cb,)), ((), ())), precision=precision, preferred_element_type=F32
    )


def iota(shape, dim):
    return lax.broadcasted_iota(jnp.int32, shape, dim)


def condense_kernel(size_ref, flex_ref, coup_ref, bound_ref, tile_ref):
    count = size_ref[pl.program_id(0)]
    interior = flex_ref.shape[1]
    masked = jnp.where(iota((interior, 1), 0) < count, coup_ref[0], jnp.zeros((), BF16))
    flexed = dot(masked, flex_ref[0], 0, 0)
    flexed = jnp.where(iota((1, interior), 1) < count, flexed, 0.0).astype(BF16)
    edge = tile_ref.shape[3]
    for a in range(4):
        cols = slice(a * edge, (a + 1) * edge)
        part = bound_ref[0, :, cols].astype(F32) - dot(flexed, masked[:, cols])
        tile_ref[0, a] = part.astype(BF16)


def condense(sizes, flexibility, coupling, boundary):
    subs, interior, order = coupling.shape
    edge = order // 4
    return pl.pallas_call(
        condense_kernel,
        out_shape=jax.ShapeDtypeStruct((subs, 4, order, edge), BF16),
        grid_spec=pltpu.PrefetchScalarGridSpec(
            num_scalar_prefetch=1,
            grid=(subs,),
            in_specs=[
                pl.BlockSpec((1, interior, interior), lambda s, n: (s, 0, 0)),
                pl.BlockSpec((1, interior, order), lambda s, n: (s, 0, 0)),
                pl.BlockSpec((1, order, order), lambda s, n: (s, 0, 0)),
            ],
            out_specs=pl.BlockSpec((1, 4, order, edge), lambda s, n: (s, 0, 0, 0)),
        ),
        name="condense",
    )(sizes, flexibility, coupling, boundary)


def lane_pick(x, k):
    return jnp.take_along_axis(x, jnp.full(x.shape, k, jnp.int32), axis=1)


def eliminate(work, subs, order):
    for k in range(order - 1):
        row = work[k]
        scaled_row = row / row[:, k : k + 1]
        tail = work[k + 1 :]
        work[k + 1 :] = tail - tail[:, :, k : k + 1] * scaled_row[None]


def subspace_kernel(
    size_ref, flex_ref, coup_ref, mass_ref, start_ref, out_ref, scaled, applied, work
):
    subs, modes, interior = start_ref.shape
    lanes = iota((1, interior), 1)
    eye = (iota((modes, modes), 0) == iota((modes, modes), 1)).astype(F32)
    diagonal = iota((modes, 128), 0) == iota((modes, 128), 1)

    def weight_of(s):
        return jnp.where(lanes < size_ref[s], mass_ref[s], 0.0)

    for s in range(subs):
        scaled[s] = (start_ref[s].astype(F32) * weight_of(s)).astype(BF16)

    def sweep(i, carry):
        for s in range(subs):
            y = jnp.where(lanes < size_ref[s], dot(scaled[s], flex_ref[s]), 0.0)
            applied[s] = y
            gram = dot(y * weight_of(s), y, 1, 1, HIGHEST)
            work[:, s] = jnp.concatenate([gram, eye], axis=1)
        eliminate(work, subs, modes)
        for s in range(subs):
            done = work[:, s]
            pivots = jnp.sum(jnp.where(diagonal, done, 0.0), axis=1, keepdims=True)
            inverse = done[:, modes:] * lax.rsqrt(pivots)
            x = dot(inverse, applied[s], 1, 0, HIGHEST)
            scaled[s] = (x * weight_of(s)).astype(BF16)
        return carry

    lax.fori_loop(0, ITERS, sweep, 0)

    for s in range(subs):
        v = jnp.where(lanes < size_ref[s], dot(scaled[s], flex_ref[s]), 0.0)
        high = v.astype(BF16)
        low = (v - high.astype(F32)).astype(BF16)
        coupled = coup_ref[s]
        out_ref[s] = -(dot(high, coupled) + dot(low, coupled))


def subspace(sizes, flexibility, coupling, masses, start_modes):
    subs, modes, interior = start_modes.shape
    order = coupling.shape[2]
    vmem = pl.BlockSpec(memory_space=pltpu.VMEM)
    return pl.pallas_call(
        subspace_kernel,
        out_shape=jax.ShapeDtypeStruct((subs, modes, order), F32),
        in_specs=[pl.BlockSpec(memory_space=pltpu.SMEM)] + [vmem] * 4,
        out_specs=vmem,
        scratch_shapes=[
            pltpu.VMEM((subs, modes, interior), BF16),
            pltpu.VMEM((subs, modes, interior), F32),
            pltpu.VMEM((modes, subs, 2 * modes), F32),
        ],
        compiler_params=pltpu.CompilerParams(vmem_limit_bytes=40 * 1024 * 1024),
        name="subspace",
    )(sizes, flexibility, coupling, masses.reshape(subs, 1, interior), start_modes)


def copy_to(axis, peer, src, dst, send, recv):
    return pltpu.make_async_remote_copy(
        src_ref=src,
        dst_ref=dst,
        send_sem=send,
        recv_sem=recv,
        device_id={axis: peer},
        device_id_type=pl.DeviceIdType.MESH,
    )


class Exchange:
    def __init__(self, axis, count, src, dst, per, sems, same=False):
        self.axis, self.count, self.src, self.dst, self.per = axis, count, src, dst, per
        self.send, self.recv, self.same = sems[0], sems[1], same
        self.me = lax.axis_index(axis)

    def part(self, ref, i):
        return ref.at[pl.ds(i * self.per, self.per)]

    def source(self, i):
        return self.src if self.same else self.part(self.src, i)

    def peer(self, i):
        return lax.rem(self.me + i, self.count)

    def start_one(self, peer):
        copy_to(
            self.axis, peer, self.source(peer), self.part(self.dst, self.me),
            self.send.at[peer], self.recv.at[self.me],
        ).start()

    def start(self):
        def body(i, c):
            self.start_one(self.peer(i))
            return c

        lax.fori_loop(1, self.count, body, 0)
        self.keep()

    def keep(self):
        mine = pl.ds(self.me * self.per, self.per)
        self.dst[mine] = self.src[...] if self.same else self.src[mine]

    def wait(self):
        def body(i, c):
            peer = self.peer(i)
            copy = copy_to(
                self.axis, peer, self.source(peer), self.part(self.dst, peer),
                self.send.at[peer], self.recv.at[peer],
            )
            copy.wait_send()
            copy.wait_recv()
            return c

        lax.fori_loop(1, self.count, body, 0)


def small_factor(work, gram):
    order = gram.shape[0]
    eye = (iota((order, order), 0) == iota((order, order), 1)).astype(F32)
    work[:, :order] = gram
    work[:, order : 2 * order] = eye
    work[:, 2 * order :] = jnp.zeros((order, 128 - 2 * order), F32)
    rows = iota((order, 128), 0)

    def body(k, carry):
        row = work[pl.ds(k, 1), :]
        pivot = lane_pick(jnp.broadcast_to(row, (8, 128)), k)[:1]
        full = work[...]
        column = jnp.where(rows > k, lane_pick(full, k), 0.0)
        work[...] = full - column * (row / pivot)
        return carry

    lax.fori_loop(0, order, body, 0)
    done = work[...]
    diagonal = rows == iota((order, 128), 1)
    pivots = jnp.sum(jnp.where(diagonal, done, 0.0), axis=1, keepdims=True)
    done = done * lax.rsqrt(pivots)
    return done[:, :order], done[:, order : 2 * order]


def lanczos_kernel(
    rescale, rows, cols,
    loc_ref, inv_sub_ref, inv_blk_ref, want_ref, start_ref, tile_ref,
    alpha1_ref, alpha2_ref, next_ref, resid_ref,
    xloc, got, pick, have, xs, out, came, part, sums, wants, pay, prow, pcol, work,
    want_smem, tiles, local_sem, tile_sem, *sems,
):
    subs = tile_ref.shape[0]
    width = start_ref.shape[0]
    edge = start_ref.shape[1] // 2
    my_row, my_col = lax.axis_index("row"), lax.axis_index("col")

    barrier = pltpu.get_barrier_semaphore()

    def greet(axis, me, count):
        def body(i, c):
            pl.semaphore_signal(
                barrier, inc=1, device_id={axis: lax.rem(me + i, count)},
                device_id_type=pl.DeviceIdType.MESH,
            )
            return c

        lax.fori_loop(1, count, body, 0)

    greet("row", my_row, rows)
    greet("col", my_col, cols)

    load = pltpu.make_async_copy(tile_ref, tiles, tile_sem)
    load.start()
    pl.semaphore_wait(barrier, rows + cols - 2)

    sems = list(sems)
    ask = Exchange("col", cols, want_ref, wants, 1, sems[0:2])
    ask.start()

    def psum(i, base):
        by_row = Exchange("row", rows, pay.at[i, 0], prow.at[i], 1, sems[base : base + 2], True)
        by_col = Exchange("col", cols, pay.at[i, 1], pcol.at[i], 1, sems[base + 2 : base + 4], True)

        def middle():
            by_row.wait()
            total = prow[i, 0]
            for r in range(1, rows):
                total = total + prow[i, r]
            pay[i, 1, 0] = total
            by_col.start()

        def end():
            by_col.wait()
            total = pcol[i, 0]
            for c in range(1, cols):
                total = total + pcol[i, c]
            return total

        return by_row.start, middle, end

    def spread(i, base):
        first = Exchange("row", rows, xloc.at[i], got.at[i], 2, sems[base : base + 2], True)
        second = Exchange("col", cols, pick.at[i], have.at[i], 4, sems[base + 2 : base + 4])

        def middle():
            first.wait()

            def choose(d, c):
                for k in range(4):
                    pick[i, 4 * d + k] = got[i, want_smem[d, k, 0]]
                return c

            lax.fori_loop(0, cols, choose, 0)
            second.start()

        def end():
            second.wait()

            def gather(s, c):
                for a in range(4):
                    xs[i, s, :, a * edge : (a + 1) * edge] = have[i, loc_ref[4 * s + a]]
                return c

            lax.fori_loop(0, subs, gather, 0)

        return first.start, middle, end

    def multiply(i, base):
        first = Exchange("col", cols, out.at[i], came.at[i], 4, sems[base : base + 2])
        second = Exchange("row", rows, part.at[i], sums.at[i], 2, sems[base + 2 : base + 4])

        def begin():
            def terms(j, c):
                d = lax.rem(my_col + 1 + j, cols)
                for k in range(4):
                    q = 4 * d + k
                    s, a = inv_sub_ref[q], inv_blk_ref[q]
                    out[i, q] = dot(xs[i, s], tiles[s, a]).astype(BF16)

                @pl.when(j < cols - 1)
                def _():
                    first.start_one(d)

                return c

            lax.fori_loop(0, cols, terms, 0)
            first.keep()

        def middle():
            first.wait()
            for h in range(width // 16):
                piece = slice(16 * h, 16 * h + 16)

                def add(c, totals):
                    totals = list(totals)
                    for k in range(4):
                        term = came[i, 4 * c + k, piece].astype(F32)
                        slot = wants[c, k : k + 1, :]
                        for t in range(2 * rows):
                            totals[t] = totals[t] + jnp.where(slot == t, term, 0.0)
                    return tuple(totals)

                zero = jnp.zeros((16, edge), F32)
                totals = lax.fori_loop(0, cols, add, (zero,) * (2 * rows))
                for t in range(2 * rows):
                    part[i, t, piece] = totals[t]
            second.start()

        def end():
            second.wait()
            halves = []
            for p in range(2):
                total = sums[i, p]
                for r in range(1, rows):
                    total = total + sums[i, 2 * r + p]
                halves.append(total)
            return jnp.concatenate(halves, axis=1)

        return begin, middle, end

    def put_vector(i, vector):
        for p in range(2):
            xloc[i, p] = vector[:, p * edge : (p + 1) * edge].astype(BF16)
        return jnp.concatenate([xloc[i, p].astype(F32) for p in range(2)], axis=1)

    zero_pad = jnp.zeros((width, 128 - width), F32)
    start = start_ref[...]
    rounded = put_vector(0, start)
    spread0, sum0 = spread(0, 2), psum(0, 6)
    spread0[0]()
    pay[0, 0, 0] = jnp.concatenate([dot(start, start, 1, 1, HIGHEST), zero_pad], axis=1)
    sum0[0]()
    ask.wait()
    fetch = pltpu.make_async_copy(wants, want_smem, local_sem)
    fetch.start()
    fetch.wait()
    spread0[1]()
    sum0[1]()
    gram = sum0[2]()[:, :width]
    _, inverse0 = small_factor(work, gram)
    q0 = dot(inverse0, rounded, 1, 0, HIGHEST)
    spread0[2]()
    load.wait()

    apply0 = multiply(0, 10)
    apply0[0]()
    apply0[1]()
    w0 = dot(inverse0, apply0[2](), 1, 0, HIGHEST)

    sum1 = psum(1, 14)
    pay[1, 0, 0] = jnp.concatenate(
        [
            dot(w0, q0, 1, 1, HIGHEST),
            dot(w0, w0, 1, 1, HIGHEST),
            dot(q0, q0, 1, 1, HIGHEST),
            jnp.zeros((width, 128 - 3 * width), F32),
        ],
        axis=1,
    )
    sum1[0]()
    sum1[1]()
    total = sum1[2]()
    alpha = total[:, :width]
    alpha1_ref[...] = alpha
    carried = dot(alpha, total[:, 2 * width : 3 * width], 1, 0, HIGHEST) - 2.0 * alpha
    rest = total[:, width : 2 * width] + dot(carried, alpha, 1, 1, HIGHEST)
    beta_t, inverse1 = small_factor(work, rest)
    q1 = dot(inverse1, w0 - dot(alpha, q0, 1, 0, HIGHEST), 1, 0, HIGHEST)
    next_ref[...] = rescale * q1
    rounded1 = put_vector(1, q1)

    spread1 = spread(1, 18)
    spread1[0]()
    back = dot(beta_t, q0, 1, 0, HIGHEST)
    spread1[1]()
    spread1[2]()
    apply1 = multiply(1, 22)
    apply1[0]()
    apply1[1]()
    w1 = apply1[2]() - back

    sum2 = psum(2, 26)
    pay[2, 0, 0] = jnp.concatenate([dot(w1, rounded1, 1, 1, HIGHEST), zero_pad], axis=1)
    sum2[0]()
    sum2[1]()
    alpha2 = sum2[2]()[:, :width]
    alpha2_ref[...] = alpha2
    resid_ref[...] = rescale * (w1 - dot(alpha2, rounded1, 1, 0, HIGHEST))


def routes(interface, rows, cols):
    ids = interface.reshape(-1)
    count = ids.shape[0]
    col = (ids // 2) % cols
    order = jnp.arange(count)
    same = (col[None, :] == col[:, None]) & (order[None, :] < order[:, None])
    loc = col * 4 + jnp.sum(same.astype(jnp.int32), axis=1)
    hit = (loc[None, :] == order[:, None]).astype(jnp.int32)
    inv = jnp.sum(hit * order[None, :], axis=1)
    slot = (ids // 2 // cols) * 2 + ids % 2
    want = jnp.sum(hit * slot[None, :], axis=1).reshape(cols, 4)
    want = jnp.broadcast_to(jnp.pad(want, ((0, 0), (0, 4)))[:, :, None], (cols, 8, 128))
    return loc, inv // 4, inv % 4, want


def lanczos(tiles, interface, start_block, rows, cols):
    subs, _, order, edge = tiles.shape
    width = start_block.shape[0]
    loc, inv_sub, inv_blk, want = routes(interface, rows, cols)
    rescale = math.sqrt(rows * cols * start_block.shape[1])
    vmem = pl.BlockSpec(memory_space=pltpu.VMEM)
    smem = pl.BlockSpec(memory_space=pltpu.SMEM)
    dma = pltpu.SemaphoreType.DMA
    col_pair, row_pair = [dma((cols,))] * 2, [dma((rows,))] * 2
    sums = row_pair + col_pair
    spreads = row_pair + col_pair
    applies = col_pair + row_pair
    return pl.pallas_call(
        functools.partial(lanczos_kernel, rescale, rows, cols),
        out_shape=(
            jax.ShapeDtypeStruct((width, width), F32),
            jax.ShapeDtypeStruct((width, width), F32),
            jax.ShapeDtypeStruct(start_block.shape, F32),
            jax.ShapeDtypeStruct(start_block.shape, F32),
        ),
        in_specs=[smem, smem, smem, vmem, vmem, pl.BlockSpec(memory_space=pl.ANY)],
        out_specs=[vmem] * 4,
        scratch_shapes=[
            pltpu.VMEM((2, 2, width, edge), BF16),
            pltpu.VMEM((2, 2 * rows, width, edge), BF16),
            pltpu.VMEM((2, 4 * cols, width, edge), BF16),
            pltpu.VMEM((2, 4 * cols, width, edge), BF16),
            pltpu.VMEM((2, subs, width, order), BF16),
            pltpu.VMEM((2, 4 * cols, width, edge), BF16),
            pltpu.VMEM((2, 4 * cols, width, edge), BF16),
            pltpu.VMEM((2, 2 * rows, width, edge), F32),
            pltpu.VMEM((2, 2 * rows, width, edge), F32),
            pltpu.VMEM((cols, 8, 128), jnp.int32),
            pltpu.VMEM((3, 2, 1, width, 128), F32),
            pltpu.VMEM((3, rows, width, 128), F32),
            pltpu.VMEM((3, cols, width, 128), F32),
            pltpu.VMEM((width, 128), F32),
            pltpu.SMEM((cols, 8, 128), jnp.int32),
            pltpu.VMEM(tiles.shape, BF16),
            dma,
            dma,
            *col_pair, *spreads, *sums, *applies, *sums, *spreads, *applies, *sums,
        ],
        compiler_params=pltpu.CompilerParams(
            collective_id=0, has_side_effects=True, vmem_limit_bytes=48 * 1024 * 1024
        ),
        name="lanczos",
    )(loc, inv_sub, inv_blk, want, start_block, tiles)


def on_device(
    flexibility, coupling, boundary, masses, start_modes, interior_sizes, interface, start_block
):
    rows, cols = lax.axis_size("row"), lax.axis_size("col")
    tiles = condense(interior_sizes, flexibility, coupling, boundary)
    alpha_first, alpha_second, next_block, residual_block = lanczos(
        tiles, interface, start_block, rows, cols
    )
    mass_coupling = subspace(interior_sizes, flexibility, coupling, masses, start_modes)
    return alpha_first, alpha_second, next_block, residual_block, mass_coupling


def solution(mesh):
    both = ("row", "col")
    return jax.shard_map(
        on_device,
        mesh=mesh,
        in_specs=(
            P(both, None, None),
            P(both, None, None),
            P(both, None, None),
            P(both, None),
            P(both, None, None),
            P(both),
            P(both, None),
            P(None, both),
        ),
        out_specs=(P(), P(), P(None, both), P(None, both), P(both, None, None)),
        check_vma=False,
    )
```

time: 1210 us -> 195 us (0.16)
  other arithmetic: 729 us -> 0.34 us
  blocking collectives: 265 us -> 0 us
  Pallas kernels: 0 us -> 188 us
  matrix products: 89.5 us -> 0 us
  local copies, waits for them, and re-layouts: 69.9 us -> 5.83 us
  starting transfers between devices: 43.9 us -> 0 us
    another operation x32 -> x0, other arithmetic: 704 us -> none  [the longest x13 376 us: condense(): factor = jnp.linalg.cholesky(gram_matrix)]
    psum x4 -> x0, blocking collectives: 265 us -> none  [the longest x1 67.3 us: on_device(): lax.psum(jnp.dot(start_block, start_block.T, precision=HIGHEST), ('row',...]
    pallas_call x0 -> x3, Pallas kernels: none -> 188 us  [the longest x1 108 us: lanczos(): pl.pallas_call(functools.partial(lanczos_kernel, rescale, rows, cols), ou...]
    dot_general x24 -> x0, matrix products: 82.2 us -> none  [the longest x1 17.3 us: condense(): jnp.dot(flexed, masked, preferred_element_type=jnp.float32)]
    all_to_all x5 -> x0, starting transfers between devices: 43.9 us -> none  [the longest x2 20.6 us: apply_matrix(): lax.all_to_all(outgoing.astype(jnp.bfloat16), ('row', 'col'), split_axis=...]
    convert_element_type x4 -> x0, other arithmetic: 23.6 us -> none  [the longest x1 14.9 us: condense(): ((condensed + condensed.T) * 0.5).astype(jnp.bfloat16)]
    sub x1 -> x0, local copies, waits for them, and re-layouts: 17.6 us -> none  [condense(): boundary.astype(jnp.float32)]
    scatter x3 -> x0, local copies, waits for them, and re-layouts: 17 us -> none  [the longest x2 16.3 us: apply_matrix(): outgoing = jnp.zeros((slot_total, width, tile_edge), jnp.float32).at[ref_...]
  transfers between devices with their start and end apart: 5 -> 0, of which waited for: 0 -> 0; matrix products, arithmetic and copies ran while one was open for 67% -> 0% of each run, Pallas kernels for 0% -> 0%
where the time goes in v1:
time: 195 us
  Pallas kernels  188 us (96%)
  local copies, waits for them, and re-layouts  5.83 us (3%)
    pallas_call x1, Pallas kernels, lanczos(): pl.pallas_call(functools.partial(lanczos_kernel, rescale, rows, cols), ou...  108 us
    pallas_call x1, Pallas kernels, subspace(): pl.pallas_call(subspace_kernel, out_shape=jax.ShapeDtypeStruct((subs, mod...  58 us
    pallas_call x1, Pallas kernels, condense(): pl.pallas_call(condense_kernel, out_shape=jax.ShapeDtypeStruct((subs, 4,...  21.9 us
    unnamed x17, local copies, waits for them, and re-layouts  5.56 us

profile of v1, /device:TPU:1, one launch (start us, length us, event | category | flops | bytes accessed | tf_op | source)
XLA Modules:
  0.0 194.7 jit_solution(10287644333805265548)
XLA Ops:
  0.6 0.8 copy.15
  1.4 0.1 reshape.157
  1.5 0.2 convert_reduce_fusion
  1.7 0.1 select_reduce_fusion
  1.9 0.1 reshape.158
  1.9 0.1 broadcast_in_dim.2.want_ref
  2.0 0.0 copy-start.3
  2.0 21.9 %condense.1.tile_ref = bf16[16,4,512,128]{3,2,1,0:T(8,128)(2,1)} custom-call(s32[16]{0:T(128)} %size_ref.3, bf16[16,384,384]{2,1,0:T(8,128)(2,1)} %flex_ref.3, bf16[16,384,512]{2,1,0:T(8,128)(2,1)} %coup_ref.3, bf16[16,512,512]{2,1,0:T(8,128)(2,1)} %bound_ref.1), custom_call_target="tpu_custom_call" | custom-call | tf_op jit(solution)/shard_map/condense/pallas_call | solution.py:43
  23.9 0.0 copy-done.3
  23.9 0.0 copy-start.5
  23.9 0.0 copy-start
  23.9 0.0 copy-start.2
  23.9 0.0 copy-start.4
  23.9 107.9 %lanczos.1 = (f32[32,32]{1,0:T(8,128)S(1)}, f32[32,32]{1,0:T(8,128)S(1)}, f32[32,256]{1,0:T(8,128)S(1)}, f32[32,256]{1,0:T(8,128)S(1)}) custom-call(s32[64]{0:T(128)S(1)} %multiply_add_fusion.loc_ref, s32[64]{0:T(128)S(1)} %get-tuple-element.18.inv_sub_ref, s32[64]{0:T(128)S(1)} %get-tuple-element.17.inv_blk_ref, ...), custom_call_target="tpu_custom_call" | custom-call | tf_op jit(solution)/shard_map/lanczos/pallas_call | solution.py:445
  131.9 0.0 copy-done.5
  131.9 0.0 copy-done
  131.9 0.0 copy-done.2
  131.9 0.0 copy-done.4
  132.0 0.0 copy-start.1
  132.0 2.3 %copy-done.1 = bf16[16,384,384]{2,1,0:T(8,128)(2,1)S(1)} copy-done((bf16[16,384,384]{2,1,0:T(8,128)(2,1)S(1)}, bf16[16,384,384]{2,1,0:T(8,128)(2,1)}, u32[]{:S(2)}) %copy-start.1) | copy-done | bytes 4718616
  134.3 58.0 %subspace.1 = f32[16,64,512]{2,1,0:T(8,128)} custom-call(s32[16]{0:T(128)S(1)} %copy-done.4, bf16[16,384,384]{2,1,0:T(8,128)(2,1)S(1)} %copy-done.1, bf16[16,384,512]{2,1,0:T(8,128)(2,1)S(1)} %copy-done, f32[16,1,384]{2,1,0:T(1,128)S(1)} %reshape.159.mass_ref, bf16[16,64,384]{2,1,0:T(8,128)(2,1)S(1)} %copy-done.2), custom_call_target="tpu_custom_call" | custom-call | tf_op jit(solution)/shard_map/subspace/pallas_call | solution.py:115
  192.3 0.6 copy.20
  192.9 0.6 copy.21
  193.5 0.6 copy.22
  194.1 0.6 copy.23
  (6 shorter events, 0.1 us)
Async XLA Ops:
  2.0 21.9 %copy-start.3 = (f32[32,256]{1,0:T(8,128)S(1)}, f32[32,256]{1,0:T(8,128)}, u32[]{:S(2)}) copy-start(f32[32,256]{1,0:T(8,128)} %start_ref.2) | copy-start | bytes 98308
  23.9 108.0 %copy-start.5 = (f32[16,384]{1,0:T(8,128)S(1)}, f32[16,384]{1,0:T(8,128)}, u32[]{:S(2)}) copy-start(f32[16,384]{1,0:T(8,128)} %param.11) | copy-start | bytes 73732
  23.9 108.0 %copy-start = (bf16[16,384,512]{2,1,0:T(8,128)(2,1)S(1)}, bf16[16,384,512]{2,1,0:T(8,128)(2,1)}, u32[]{:S(2)}) copy-start(bf16[16,384,512]{2,1,0:T(8,128)(2,1)} %coup_ref.3) | copy-start | bytes 18874372
  23.9 108.0 %copy-start.2 = (bf16[16,64,384]{2,1,0:T(8,128)(2,1)S(1)}, bf16[16,64,384]{2,1,0:T(8,128)(2,1)}, u32[]{:S(2)}) copy-start(bf16[16,64,384]{2,1,0:T(8,128)(2,1)} %start_ref.3) | copy-start | bytes 2359300
  23.9 108.0 %copy-start.4 = (s32[16]{0:T(128)S(1)}, s32[16]{0:T(128)}, u32[]{:S(2)}) copy-start(s32[16]{0:T(128)} %size_ref.3) | copy-start | bytes 196
  132.0 2.3 %copy-start.1 = (bf16[16,384,384]{2,1,0:T(8,128)(2,1)S(1)}, bf16[16,384,384]{2,1,0:T(8,128)(2,1)}, u32[]{:S(2)}) copy-start(bf16[16,384,384]{2,1,0:T(8,128)(2,1)} %flex_ref.3) | copy-start | bytes 14155780

commit v2 on v1

v2 whole, which is shorter than its diff:
```python
import functools
import math

import jax
import jax.numpy as jnp
from jax import lax
from jax.experimental import pallas as pl
from jax.experimental.pallas import tpu as pltpu
from jax.sharding import PartitionSpec as P

ITERS = 4
HIGHEST = lax.Precision.HIGHEST
F32 = jnp.float32
BF16 = jnp.bfloat16
FILL = (3, 3, 3, 4, 3, 4, 3)
START = (2, 6, 11)


def dot(a, b, ca=1, cb=0, precision=None):
    return lax.dot_general(
        a, b, (((ca,), (cb,)), ((), ())), precision=precision, preferred_element_type=F32
    )


def iota(shape, dim):
    return lax.broadcasted_iota(jnp.int32, shape, dim)


def condense(s, size_ref, flex, coup, bound, tiles):
    interior, edge = flex.shape[1], tiles.shape[3]
    keep = iota((interior, 1), 0) < size_ref[s]
    masked = jnp.where(keep, coup[s], jnp.zeros((), BF16))
    flexed = jnp.where(keep, dot(flex[s], masked), 0.0).astype(BF16)
    for a in range(0, 4, 2):
        cols = slice(a * edge, (a + 2) * edge)
        part = (bound[s, :, cols].astype(F32) - dot(masked, flexed[:, cols], 0, 0)).astype(BF16)
        tiles[s, a] = part[:, :edge]
        tiles[s, a + 1] = part[:, edge:]
    eye = iota((edge, edge), 0) == iota((edge, edge), 1)
    total = jnp.zeros((1, edge), F32)
    for a in range(4):
        block = tiles[s, a, a * edge : (a + 1) * edge].astype(F32)
        total = total + jnp.sum(jnp.where(eye, block, 0.0), axis=0, keepdims=True)
    return total


def lane_pick(x, k):
    return jnp.take_along_axis(x, jnp.full(x.shape, k, jnp.int32), axis=1)


def split(x):
    high = x.astype(BF16)
    return high, (x - high.astype(F32)).astype(BF16)


def eliminate(work, first, last, order):
    half = iota((8, 128), 1) // order * order
    for k in range(first, last):
        at = half + k
        row = work[8 * k : 8 * k + 8]
        scaled_row = row / jnp.take_along_axis(row, at, axis=1)
        here = iota((8, 128), 1) == at
        scaled_row = jnp.where(here, scaled_row / row, scaled_row)
        for i in range(k + 1, order):
            line = work[8 * i : 8 * i + 8]
            factor = jnp.take_along_axis(line, at, axis=1)
            work[8 * i : 8 * i + 8] = jnp.where(here, 0.0, line) - factor * scaled_row


def weight_of(size_ref, mass_ref, s):
    lanes = iota((1, mass_ref.shape[1]), 1)
    return jnp.where(lanes < size_ref[s], mass_ref[s : s + 1], 0.0)


def active(size_ref, s, x):
    return jnp.where(iota((1, x.shape[1]), 1) < size_ref[s], x, 0.0)


def sub_begin(size_ref, mass_ref, start_ref, scaled):
    for s in range(start_ref.shape[0]):
        start = start_ref[s].astype(F32)
        scaled[s] = (start * weight_of(size_ref, mass_ref, s)).astype(BF16)


def sub_before(j, size_ref, flex_ref, mass_ref, scaled, applied, work):
    grams = []
    for s in (j, j + 8):
        y = active(size_ref, s, dot(scaled[s], flex_ref[s]))
        high, low = split(y)
        modes = y.shape[0]
        applied[s, :modes] = high
        applied[s, modes : 2 * modes] = low
        applied[s, 2 * modes :] = high
        left, left_low = split(y * weight_of(size_ref, mass_ref, s))
        grams.append(
            dot(
                jnp.concatenate([left, left, left_low], axis=1),
                jnp.concatenate([high, low, high], axis=1),
                1,
                1,
            )
        )
    work[pl.ds(j, grams[0].shape[0], stride=8), :] = jnp.concatenate(grams, axis=1)


def sub_after(j, size_ref, mass_ref, scaled, applied, work):
    modes = scaled.shape[1]
    both = work[pl.ds(j, modes, stride=8), :]
    lower, row = iota((modes, modes), 1), iota((modes, modes), 0)
    for h in range(2):
        s = j + 8 * h
        done = both[:, h * modes : (h + 1) * modes]
        pivots = jnp.sum(jnp.where(lower == row, done, 0.0), axis=1, keepdims=True)
        inverse = jnp.where(lower < row, done, jnp.where(lower == row, 1.0, 0.0))
        high, low = split(inverse * lax.rsqrt(pivots))
        x = dot(jnp.concatenate([high, high, low], axis=1), applied[s])
        scaled[s] = (x * weight_of(size_ref, mass_ref, s)).astype(BF16)


def sub_last(s, size_ref, flex_ref, coup_ref, scaled, out_ref):
    modes = scaled.shape[1]
    high, low = split(active(size_ref, s, dot(scaled[s], flex_ref[s])))
    both = dot(jnp.concatenate([high, low], axis=0), coup_ref[s])
    out_ref[s] = -(both[:modes] + both[modes:])


def copy_to(axis, peer, src, dst, send, recv):
    return pltpu.make_async_remote_copy(
        src_ref=src,
        dst_ref=dst,
        send_sem=send,
        recv_sem=recv,
        device_id={axis: peer},
        device_id_type=pl.DeviceIdType.MESH,
    )


class Exchange:
    def __init__(self, axis, count, src, dst, per, sems, same=False):
        self.axis, self.count, self.src, self.dst, self.per = axis, count, src, dst, per
        self.send, self.recv, self.same = sems[0], sems[1], same
        self.me = lax.axis_index(axis)

    def part(self, ref, i):
        return ref.at[pl.ds(i * self.per, self.per)]

    def source(self, i):
        return self.src if self.same else self.part(self.src, i)

    def peer(self, i):
        return lax.rem(self.me + i, self.count)

    def start_one(self, peer):
        copy_to(
            self.axis, peer, self.source(peer), self.part(self.dst, self.me),
            self.send.at[peer], self.recv.at[self.me],
        ).start()

    def start(self):
        def body(i, c):
            self.start_one(self.peer(i))
            return c

        lax.fori_loop(1, self.count, body, 0)
        self.keep()

    def keep(self):
        mine = pl.ds(self.me * self.per, self.per)
        self.dst[mine] = self.src[...] if self.same else self.src[mine]

    def described(self, peer):
        return copy_to(
            self.axis, peer, self.source(peer), self.part(self.dst, peer),
            self.send.at[peer], self.recv.at[peer],
        )

    def wait_recv(self, peer):
        self.described(peer).wait_recv()

    def wait_sends(self):
        def body(i, c):
            self.described(self.peer(i)).wait_send()
            return c

        lax.fori_loop(1, self.count, body, 0)

    def wait(self):
        def body(i, c):
            self.wait_recv(self.peer(i))
            return c

        lax.fori_loop(1, self.count, body, 0)
        self.wait_sends()


def small_factor(gram):
    order = gram.shape[0]
    rows, lanes = iota((order, 128), 0), iota((order, 128), 1)
    eye = (iota((order, order), 0) == iota((order, order), 1)).astype(F32)
    x = jnp.concatenate([gram, eye, jnp.zeros((order, 128 - 2 * order), F32)], axis=1)
    for k in range(order - 1):
        row = x[k : k + 1]
        column = jnp.where(rows > k, x[:, k : k + 1], 0.0)
        x = x - column * (row / row[:, k : k + 1])
    pivots = jnp.sum(jnp.where(rows == lanes, x, 0.0), axis=1, keepdims=True)
    x = x * lax.rsqrt(pivots)
    return x[:, :order], x[:, order : 2 * order]


def whole_kernel(
    rescale, rows, cols,
    size_ref, loc_ref, inv_sub_ref, inv_blk_ref, want_ref, start_ref, mass_ref, modes_ref,
    flex_ref, coup_ref, bound_ref,
    small_ref, mass_out_ref,
    xloc, got, pick, have, xs, out, came, part, sums, ask_rows, wants,
    pay, prow, pcol, pay_s, prow_s, pcol_s,
    want_smem, tiles, flex, coup, bound, scaled, applied, work,
    local_sem, load_sem, *sems,
):
    subs, order = bound_ref.shape[:2]
    width = start_ref.shape[0]
    modes = modes_ref.shape[1]
    edge = start_ref.shape[1] // 2
    my_row, my_col = lax.axis_index("row"), lax.axis_index("col")

    barrier = pltpu.get_barrier_semaphore()

    def greet(axis, me, count):
        def body(i, c):
            pl.semaphore_signal(
                barrier, inc=1, device_id={axis: lax.rem(me + i, count)},
                device_id_type=pl.DeviceIdType.MESH,
            )
            return c

        lax.fori_loop(1, count, body, 0)

    greet("row", my_row, rows)
    greet("col", my_col, cols)

    def loads(s):
        pairs = ((flex_ref, flex), (coup_ref, coup), (bound_ref, bound))
        return [
            pltpu.make_async_copy(far.at[s], near.at[s], load_sem.at[n, s])
            for n, (far, near) in enumerate(pairs)
        ]

    def load_all(s, c):
        for load in loads(s):
            load.start()
        return c

    lax.fori_loop(0, subs, load_all, 0)

    def condense_some(first, last):
        def body(s, c):
            for load in loads(s):
                load.wait()
            return c + condense(s, size_ref, flex, coup, bound, tiles)

        return lax.fori_loop(first, last, body, jnp.zeros((1, edge), F32))

    def pieces():
        for _ in range(ITERS):
            for j in range(8):
                sub_before(j, size_ref, flex, mass_ref, scaled, applied, work)
            yield
            for cut in range(0, modes, modes // 4):
                eliminate(work, cut, min(cut + modes // 4, modes - 1), modes)
                yield
            for j in range(8):
                sub_after(j, size_ref, mass_ref, scaled, applied, work)
            yield
        for h in range(2):
            for s in range(h * subs // 2, (h + 1) * subs // 2):
                sub_last(s, size_ref, flex, coup, scaled, mass_out_ref)
            yield

    queue = pieces()

    def fill(count):
        for _ in range(count):
            next(queue, None)

    sems = list(sems)
    def fill_wants(d, c):
        for k in range(4):
            ask_rows[d, k : k + 1, :] = jnp.full((1, 128), want_ref[4 * d + k], jnp.int32)
        ask_rows[d, 4:, :] = jnp.zeros((4, 128), jnp.int32)
        return c

    lax.fori_loop(0, cols, fill_wants, 0)
    ask = Exchange("col", cols, ask_rows, wants, 1, sems[0:2])

    def psum(pay, prow, pcol, i, base):
        by_row = Exchange("row", rows, pay.at[i, 0], prow.at[i], 1, sems[base : base + 2], True)
        by_col = Exchange("col", cols, pay.at[i, 1], pcol.at[i], 1, sems[base + 2 : base + 4], True)

        def middle():
            by_row.wait()
            total = prow[i, 0]
            for r in range(1, rows):
                total = total + prow[i, r]
            pay[i, 1, 0] = total
            by_col.start()

        def end():
            by_col.wait()
            total = pcol[i, 0]
            for c in range(1, cols):
                total = total + pcol[i, c]
            return total

        return by_row.start, middle, end

    def spread(i, base):
        first = Exchange("row", rows, xloc.at[i], got.at[i], 2, sems[base : base + 2], True)
        second = Exchange("col", cols, pick.at[i], have.at[i], 4, sems[base + 2 : base + 4])

        def middle():
            first.wait()

            def choose(j, c):
                d = lax.rem(my_col + 1 + j, cols)

                @pl.when(j > 0)
                def _():
                    second.start_one(lax.rem(my_col + j, cols))

                for k in range(4):
                    pick[i, 4 * d + k] = got[i, want_smem[d, k, 0]]
                return c

            lax.fori_loop(0, cols, choose, 0)
            second.keep()

        def end():
            second.wait()

            def gather(s, c):
                for a in range(4):
                    xs[i, s, :, a * edge : (a + 1) * edge] = have[i, loc_ref[4 * s + a]]
                return c

            lax.fori_loop(0, subs, gather, 0)

        return first.start, middle, end

    def multiply(i, base):
        first = Exchange("col", cols, out.at[i], came.at[i], 4, sems[base : base + 2])
        second = Exchange("row", rows, part.at[i], sums.at[i], 2, sems[base + 2 : base + 4])

        def begin():
            def terms(j, c):
                d = lax.rem(my_col + 1 + j, cols)

                @pl.when(j > 0)
                def _():
                    first.start_one(lax.rem(my_col + j, cols))

                for k in range(4):
                    q = 4 * d + k
                    s, a = inv_sub_ref[q], inv_blk_ref[q]
                    out[i, q] = dot(xs[i, s], tiles[s, a]).astype(BF16)
                return c

            lax.fori_loop(0, cols, terms, 0)
            first.keep()

        def add(c, fresh):
            for h in range(width // 16):
                piece = slice(16 * h, 16 * h + 16)
                terms = [came[i, 4 * c + k, piece].astype(F32) for k in range(4)]
                slots = [wants[c, k : k + 1, :] for k in range(4)]
                for t in range(2 * rows):
                    total = jnp.zeros((16, edge), F32) if fresh else part[i, t, piece]
                    for k in range(4):
                        total = total + jnp.where(slots[k] == t, terms[k], 0.0)
                    part[i, t, piece] = total

        def middle():
            add(my_col, True)

            def take(j, c):
                first.wait_recv(lax.rem(my_col + cols - j, cols))
                add(lax.rem(my_col + cols - j, cols), False)
                return c

            lax.fori_loop(1, cols, take, 0)
            second.start()
            first.wait_sends()

        def end():
            second.wait()
            halves = []
            for p in range(2):
                total = sums[i, p]
                for r in range(1, rows):
                    total = total + sums[i, 2 * r + p]
                halves.append(total)
            return jnp.concatenate(halves, axis=1)

        return begin, middle, end

    def put_vector(i, vector):
        for p in range(2):
            xloc[i, p] = vector[:, p * edge : (p + 1) * edge].astype(BF16)
        return jnp.concatenate([xloc[i, p].astype(F32) for p in range(2)], axis=1)

    def fold(x):
        return jnp.concatenate([x[8 * g : 8 * g + 8] for g in range(width // 8)], axis=1)

    def unfold(x):
        return jnp.concatenate(
            [x[:, width * g : width * g + width] for g in range(width // 8)], axis=0
        )

    def high(a, b, ca=1, cb=0):
        return dot(a, b, ca, cb, HIGHEST)

    pad = jnp.zeros((width, 128 - 2 * width), F32)
    start = start_ref[...]
    rounded = put_vector(0, start)
    spread0, sum0 = spread(0, 2), psum(pay, prow, pcol, 0, 6)
    grams = [high(start, start, 1, 1), high(rounded, rounded, 1, 1), pad]
    pay[0, 0, 0] = jnp.concatenate(grams, axis=1)
    trace = condense_some(0, START[0])
    pl.semaphore_wait(barrier, rows + cols - 2)
    ask.start()
    spread0[0]()
    sum0[0]()
    sub_begin(size_ref, mass_ref, modes_ref, scaled)
    trace = trace + condense_some(START[0], START[1])
    ask.wait()
    fetch = pltpu.make_async_copy(wants, want_smem, local_sem)
    fetch.start()
    fetch.wait()
    spread0[1]()
    sum0[1]()
    trace = trace + condense_some(START[1], START[2])
    grams = sum0[2]()
    _, inverse0 = small_factor(grams[:, :width])
    q0 = high(inverse0, rounded)
    norm0 = high(high(inverse0, grams[:, width : 2 * width]), inverse0, 1, 1)
    trace = trace + condense_some(START[2], subs)
    sum_t = psum(pay_s, prow_s, pcol_s, 0, 14)
    pay_s[0, 0, 0] = jnp.broadcast_to(trace, (8, edge))
    sum_t[0]()
    spread0[2]()

    apply0 = multiply(0, 10)
    apply0[0]()
    fill(FILL[0])
    sum_t[1]()
    apply0[1]()
    fill(FILL[1])
    shift = jnp.sum(sum_t[2]()[:1], axis=1, keepdims=True) / (rows * cols * 2 * edge)
    image = apply0[2]()
    moved = image - shift * rounded
    moved_rounded = put_vector(1, moved)
    spread1 = spread(1, 18)
    spread1[0]()

    v0 = high(inverse0, moved_rounded)
    sum1 = psum(pay, prow, pcol, 1, 22)
    pay[1, 0, 0] = jnp.concatenate([high(v0, q0, 1, 1), high(v0, v0, 1, 1), pad], axis=1)
    sum1[0]()
    w0 = high(inverse0, image)
    v0_full = high(inverse0, moved)
    fill(FILL[2])
    spread1[1]()
    sum1[1]()
    fill(FILL[3])
    spread1[2]()
    apply1 = multiply(1, 26)
    apply1[0]()

    total = sum1[2]()
    cross, square = total[:, :width], total[:, width : 2 * width]
    eye = (iota((width, width), 0) == iota((width, width), 1)).astype(F32)
    alpha = cross + shift * norm0
    less = alpha - shift * eye
    across = high(less, cross, 1, 1)
    rest = square - across - high(cross, less, 1, 1) + high(high(less, norm0), less, 1, 1)
    beta_t, inverse1 = small_factor(rest)
    off = high(less, q0)
    small_ref[:, : 2 * edge] = rescale * high(inverse1, v0_full - off)
    q1 = high(inverse1, v0 - off)
    known = high(inverse1, high(less, w0)) + high(beta_t, q0)
    both_inverse = high(inverse1, inverse0)
    fill(FILL[4])
    apply1[1]()
    fill(FILL[5])
    w1 = high(both_inverse, apply1[2]()) - known

    sum2 = psum(pay_s, prow_s, pcol_s, 1, 30)
    pay_s[1, 0, 0] = fold(high(w1, q1, 1, 1))
    sum2[0]()
    fill(FILL[6])
    sum2[1]()
    fill(100)
    alpha2 = unfold(sum2[2]())
    small_ref[:, 2 * edge : 4 * edge] = rescale * (w1 - high(alpha2, q1))
    small_ref[:, 4 * edge :] = jnp.concatenate([alpha, alpha2, pad], axis=1)


def finish_kernel(
    small_ref, mass_ref, alpha1_ref, alpha2_ref, next_ref, resid_ref, mass_out_ref
):
    width, length = next_ref.shape
    mass_out_ref[...] = mass_ref[...]
    next_ref[...] = small_ref[:, :length]
    resid_ref[...] = small_ref[:, length : 2 * length]
    alpha1_ref[...] = small_ref[:, 2 * length : 2 * length + width]
    alpha2_ref[...] = small_ref[:, 2 * length + width : 2 * length + 2 * width]


def routes(interface, rows, cols):
    ids = interface.reshape(-1)
    count = ids.shape[0]
    col = (ids // 2) % cols
    order = jnp.arange(count)
    same = (col[None, :] == col[:, None]) & (order[None, :] < order[:, None])
    loc = col * 4 + jnp.sum(same.astype(jnp.int32), axis=1)
    hit = (loc[None, :] == order[:, None]).astype(jnp.int32)
    inv = jnp.sum(hit * order[None, :], axis=1)
    slot = (ids // 2 // cols) * 2 + ids % 2
    want = jnp.sum(hit * slot[None, :], axis=1)
    return loc, inv // 4, inv % 4, want


def on_device(
    flexibility, coupling, boundary, masses, start_modes, interior_sizes, interface, start_block
):
    rows, cols = lax.axis_size("row"), lax.axis_size("col")
    subs, interior, order = coupling.shape
    modes = start_modes.shape[1]
    width = start_block.shape[0]
    edge = order // 4
    loc, inv_sub, inv_blk, want = routes(interface, rows, cols)
    rescale = math.sqrt(rows * cols * start_block.shape[1])
    vmem = pl.BlockSpec(memory_space=pltpu.VMEM)
    smem = pl.BlockSpec(memory_space=pltpu.SMEM)
    far = pl.BlockSpec(memory_space=pl.ANY)
    dma = pltpu.SemaphoreType.DMA
    col_pair, row_pair = [dma((cols,))] * 2, [dma((rows,))] * 2
    sums = row_pair + col_pair
    spreads = row_pair + col_pair
    applies = col_pair + row_pair
    small, mass_coupling = pl.pallas_call(
        functools.partial(whole_kernel, rescale, rows, cols),
        out_shape=(
            jax.ShapeDtypeStruct((width, 5 * edge), F32),
            jax.ShapeDtypeStruct((subs, modes, order), F32),
        ),
        in_specs=[smem] * 5 + [vmem] * 3 + [far] * 3,
        out_specs=[vmem] * 2,
        scratch_shapes=[
            pltpu.VMEM((2, 2, width, edge), BF16),
            pltpu.VMEM((2, 2 * rows, width, edge), BF16),
            pltpu.VMEM((2, 4 * cols, width, edge), BF16),
            pltpu.VMEM((2, 4 * cols, width, edge), BF16),
            pltpu.VMEM((2, subs, width, order), BF16),
            pltpu.VMEM((2, 4 * cols, width, edge), BF16),
            pltpu.VMEM((2, 4 * cols, width, edge), BF16),
            pltpu.VMEM((2, 2 * rows, width, edge), F32),
            pltpu.VMEM((2, 2 * rows, width, edge), F32),
            pltpu.VMEM((cols, 8, 128), jnp.int32),
            pltpu.VMEM((cols, 8, 128), jnp.int32),
            pltpu.VMEM((2, 2, 1, width, 128), F32),
            pltpu.VMEM((2, rows, width, 128), F32),
            pltpu.VMEM((2, cols, width, 128), F32),
            pltpu.VMEM((2, 2, 1, 8, 128), F32),
            pltpu.VMEM((2, rows, 8, 128), F32),
            pltpu.VMEM((2, cols, 8, 128), F32),
            pltpu.SMEM((cols, 8, 128), jnp.int32),
            pltpu.VMEM((subs, 4, order, edge), BF16),
            pltpu.VMEM(flexibility.shape, BF16),
            pltpu.VMEM(coupling.shape, BF16),
            pltpu.VMEM(boundary.shape, BF16),
            pltpu.VMEM((subs, modes, interior), BF16),
            pltpu.VMEM((subs, 3 * modes, interior), BF16),
            pltpu.VMEM((8 * modes, 2 * modes), F32),
            dma,
            dma((3, subs)),
            *col_pair, *spreads, *sums, *applies, *sums, *spreads, *sums, *applies, *sums,
        ],
        compiler_params=pltpu.CompilerParams(
            collective_id=0, has_side_effects=True, vmem_limit_bytes=56 * 1024 * 1024
        ),
        name="whole",
    )(
        interior_sizes, loc, inv_sub, inv_blk, want, start_block,
        masses, start_modes, flexibility, coupling, boundary,
    )
    steps = 4
    once = lambda shape: pl.BlockSpec(shape, lambda g: (0, 0))
    slab = pl.BlockSpec((subs // steps, modes, order), lambda g: (g, 0, 0))
    return pl.pallas_call(
        finish_kernel,
        grid=(steps,),
        out_shape=(
            jax.ShapeDtypeStruct((width, width), F32),
            jax.ShapeDtypeStruct((width, width), F32),
            jax.ShapeDtypeStruct(start_block.shape, F32),
            jax.ShapeDtypeStruct(start_block.shape, F32),
            jax.ShapeDtypeStruct((subs, modes, order), F32),
        ),
        in_specs=[once(small.shape), slab],
        out_specs=[once((width, width))] * 2 + [once(start_block.shape)] * 2 + [slab],
        name="finish",
    )(small, mass_coupling)


def solution(mesh):
    both = ("row", "col")
    return jax.shard_map(
        on_device,
        mesh=mesh,
        in_specs=(
            P(both, None, None),
            P(both, None, None),
            P(both, None, None),
            P(both, None),
            P(both, None, None),
            P(both),
            P(both, None),
            P(None, both),
        ),
        out_specs=(P(), P(), P(None, both), P(None, both), P(both, None, None)),
        check_vma=False,
    )
```

time: 195 us -> 111 us (0.57)
  Pallas kernels: 188 us -> 108 us
  local copies, waits for them, and re-layouts: 5.83 us -> 0.85 us
    pallas_call x3 -> x2, Pallas kernels: 188 us -> 108 us  [the longest x1 104 us: on_device(): pl.pallas_call(functools.partial(whole_kernel, rescale, rows, cols), out_...]
    unnamed x17 -> x3, local copies, waits for them, and re-layouts: 5.56 us -> 0.77 us
where the time goes in v2:
time: 111 us
  Pallas kernels  108 us (97%)
  other arithmetic  1.37 us (1%)
    pallas_call x1, Pallas kernels, on_device(): pl.pallas_call(functools.partial(whole_kernel, rescale, rows, cols), out_...  104 us
    pallas_call x1, Pallas kernels, on_device(): pl.pallas_call(finish_kernel, grid=(steps,), out_shape=(jax.ShapeDtypeStr...  3.81 us

profile of v2, /device:TPU:1, one launch (start us, length us, event | category | flops | bytes accessed | tf_op | source)
XLA Modules:
  0.0 110.8 jit_solution(17616644172009864786)
XLA Ops:
  0.6 0.8 copy.15
  1.4 0.1 reshape.150
  1.5 0.2 convert_reduce_fusion
  1.7 0.0 copy-start
  1.7 0.6 select_reduce_fusion
  2.4 0.5 and_select_fusion.2
  2.9 0.0 copy-done
  2.9 104.0 %whole.1 = (f32[32,640]{1,0:T(8,128)}, f32[16,64,512]{2,1,0:T(8,128)}) custom-call(s32[16]{0:T(128)} %size_ref.1, s32[64]{0:T(128)} %copy-done, s32[64]{0:T(128)} %get-tuple-element.14.inv_sub_ref, s32[64]{0:T(128)} %get-tuple-element.13.inv_blk_ref, s32[64]{0:T(128)} %get-tuple-element.9.want_ref, f32[32,256]{1,0:T(8,128)} %start_ref.1, ...), custom_call_target="tpu_custom_call" | custom-call | tf_op jit(solution)/shard_map/whole/pallas_call | solution.py:550
  106.9 3.8 %finish.1 = (f32[32,32]{1,0:T(8,128)}, f32[32,32]{1,0:T(8,128)}, f32[32,256]{1,0:T(8,128)}, f32[32,256]{1,0:T(8,128)}, f32[16,64,512]{2,1,0:T(8,128)}) custom-call(f32[32,640]{1,0:T(8,128)} %get-tuple-element.7.small_ref, f32[16,64,512]{2,1,0:T(8,128)} %get-tuple-element.8.mass_ref), custom_call_target="tpu_custom_call" | custom-call | tf_op jit(solution)/shard_map/finish/pallas_call | solution.py:599
  (3 shorter events, 0.0 us)
Async XLA Ops:
  1.7 1.2 %copy-start = (s32[64]{0:T(128)}, s32[64]{0:T(128)S(1)}, u32[]{:S(2)}) copy-start(s32[64]{0:T(128)S(1)} %multiply_add_fusion.loc_ref) | copy-start | bytes 772

commit v3 on v2

--- a/solution.py
+++ b/solution.py
@@ -12,7 +12,7 @@
 HIGHEST = lax.Precision.HIGHEST
 F32 = jnp.float32
 BF16 = jnp.bfloat16
-FILL = (3, 3, 3, 4, 3, 4, 3)
+FILL = (3, 3, 3, 4, 1, 3, 2)
 START = (2, 6, 11)
 
 
@@ -53,18 +53,44 @@
     return high, (x - high.astype(F32)).astype(BF16)
 
 
+PIVOTS = 2
+
+
 def eliminate(work, first, last, order):
-    half = iota((8, 128), 1) // order * order
-    for k in range(first, last):
-        at = half + k
-        row = work[8 * k : 8 * k + 8]
-        scaled_row = row / jnp.take_along_axis(row, at, axis=1)
-        here = iota((8, 128), 1) == at
-        scaled_row = jnp.where(here, scaled_row / row, scaled_row)
-        for i in range(k + 1, order):
+    lanes = iota((8, 128), 1)
+    half = lanes // order * order
+    for base in range(first, last, PIVOTS):
+        span = range(PIVOTS)
+        at = [half + base + q for q in span]
+        here = [lanes == at[q] for q in span]
+        lines = [work[8 * (base + q) : 8 * (base + q) + 8] for q in span]
+        entry = [[jnp.take_along_axis(lines[q], at[r], axis=1) for r in span] for q in span]
+        scaled_rows = []
+        for q in span:
+            scale = 1.0 / entry[q][q]
+            scaled_row = jnp.where(here[q], scale, lines[q] * scale)
+            for r in range(q + 1, PIVOTS):
+                entry[q][r] = entry[q][r] * scale
+            for p in range(q + 1, PIVOTS):
+                factor = entry[p][q]
+                lines[p] = jnp.where(here[q], 0.0, lines[p]) - factor * scaled_row
+                for r in range(q + 1, PIVOTS):
+                    entry[p][r] = entry[p][r] - factor * entry[q][r]
+            for r in range(q + 1, PIVOTS):
+                scaled_row = jnp.where(here[r], 0.0, scaled_row)
+            scaled_rows.append(scaled_row)
+        for q in range(1, PIVOTS):
+            work[8 * (base + q) : 8 * (base + q) + 8] = lines[q]
+        inside = (lanes >= at[0]) & (lanes <= at[PIVOTS - 1])
+        for i in range(base + PIVOTS, order):
             line = work[8 * i : 8 * i + 8]
-            factor = jnp.take_along_axis(line, at, axis=1)
-            work[8 * i : 8 * i + 8] = jnp.where(here, 0.0, line) - factor * scaled_row
+            factors = [jnp.take_along_axis(line, at[q], axis=1) for q in span]
+            line = jnp.where(inside, 0.0, line)
+            for q in span:
+                for p in range(q):
+                    factors[q] = factors[q] - factors[p] * entry[p][q]
+                line = line - factors[q] * scaled_rows[q]
+            work[8 * i : 8 * i + 8] = line
 
 
 def weight_of(size_ref, mass_ref, s):
@@ -265,8 +291,8 @@
             for j in range(8):
                 sub_before(j, size_ref, flex, mass_ref, scaled, applied, work)
             yield
-            for cut in range(0, modes, modes // 4):
-                eliminate(work, cut, min(cut + modes // 4, modes - 1), modes)
+            for first, last in ((0, 12), (12, 28), (28, modes)):
+                eliminate(work, first, last, modes)
                 yield
             for j in range(8):
                 sub_after(j, size_ref, mass_ref, scaled, applied, work)

time: 111 us -> 113 us (1.018)
  Pallas kernels: 108 us -> 110 us
    pallas_call x1, Pallas kernels: 104 us -> 106 us  [on_device(): pl.pallas_call(functools.partial(whole_kernel, rescale, rows, cols), out_...]
where the time goes in v3:
time: 113 us
  Pallas kernels  110 us (97%)
  other arithmetic  1.37 us (1%)
    pallas_call x1, Pallas kernels, on_device(): pl.pallas_call(functools.partial(whole_kernel, rescale, rows, cols), out_...  106 us
    pallas_call x1, Pallas kernels, on_device(): pl.pallas_call(finish_kernel, grid=(steps,), out_shape=(jax.ShapeDtypeStr...  3.81 us

profile of v3, /device:TPU:1, one launch (start us, length us, event | category | flops | bytes accessed | tf_op | source)
XLA Modules:
  0.0 113.0 jit_solution(17631853404676826148)
XLA Ops:
  0.6 0.8 copy.15
  1.4 0.1 reshape.150
  1.5 0.2 convert_reduce_fusion
  1.7 0.0 copy-start
  1.7 0.6 select_reduce_fusion
  2.4 0.5 and_select_fusion.2
  2.9 0.0 copy-done
  2.9 106.2 %whole.1 = (f32[32,640]{1,0:T(8,128)}, f32[16,64,512]{2,1,0:T(8,128)}) custom-call(s32[16]{0:T(128)} %size_ref.1, s32[64]{0:T(128)} %copy-done, s32[64]{0:T(128)} %get-tuple-element.14.inv_sub_ref, s32[64]{0:T(128)} %get-tuple-element.13.inv_blk_ref, s32[64]{0:T(128)} %get-tuple-element.9.want_ref, f32[32,256]{1,0:T(8,128)} %start_ref.1, ...), custom_call_target="tpu_custom_call" | custom-call | tf_op jit(solution)/shard_map/whole/pallas_call | solution.py:576
  109.0 3.8 %finish.1 = (f32[32,32]{1,0:T(8,128)}, f32[32,32]{1,0:T(8,128)}, f32[32,256]{1,0:T(8,128)}, f32[32,256]{1,0:T(8,128)}, f32[16,64,512]{2,1,0:T(8,128)}) custom-call(f32[32,640]{1,0:T(8,128)} %get-tuple-element.7.small_ref, f32[16,64,512]{2,1,0:T(8,128)} %get-tuple-element.8.mass_ref), custom_call_target="tpu_custom_call" | custom-call | tf_op jit(solution)/shard_map/finish/pallas_call | solution.py:625
  (3 shorter events, 0.0 us)
Async XLA Ops:
  1.7 1.2 %copy-start = (s32[64]{0:T(128)}, s32[64]{0:T(128)S(1)}, u32[]{:S(2)}) copy-start(s32[64]{0:T(128)S(1)} %multiply_add_fusion.loc_ref) | copy-start | bytes 772
